TPU v7x, 32 devices: a whole 2x2x4 slice. The times are simulated.
32 devices in a mesh: dom: 16 (over z, y, x), spin: 2 (over core).
Axes of the slice: x: 2, y: 2, z: 4, core: 2. Of those that a mesh axis runs over, the one named last changes fastest.
Arguments:
- vectors: float32 [2, 8, 262144], P('spin', None, 'dom'), may hold values from -17 to 17
- basis: float32 [2, 16, 262144], P('spin', None, 'dom'), may hold values from -17 to 17
- potential: float32 [2, 262144], P('spin', 'dom'), may hold values from 1 to 3
- hop_table: bfloat16 [8, 128, 128], replicated, may hold values from -0.25 to 0.25
- soc_table: bfloat16 [2, 128, 128], replicated, may hold values from -0.5 to 0.5
- nbr_block: int32 [2048, 16], P('dom'), may hold values from 0 to 2047, as said below
- nbr_type: int32 [2048, 16], P('dom'), may hold values from 0 to 7
- nbr_count: int32 [2048], P('dom'), may hold values from 1 to 16, as said below
- flip_block: int32 [2048], P('dom'), may hold values from 0 to 2047, as said below
Outputs:
- block_one: float32 [2, 8, 262144], P('spin', None, 'dom')
- block_two: float32 [2, 8, 262144], P('spin', None, 'dom')
- coefs_one: float32 [32, 8], replicated
- coefs_two: float32 [40, 8], replicated
Inputs may be any that keep to these rules, and one draw needn't show every extreme that they name: nbr_block[i, l] equals i + d modulo 2048 with -8 <= d <= 8; slots at or beyond nbr_count[i] are ignored; in slot 0, the first block of each group of 128 has d = -8 and the last has d = 8. `nbr_count`: some block has all 16 slots live. flip_block[i] lies in the same domain as i: flip_block[i] // 128 == i // 128.
All inputs are finite; a program needn't handle non-finite values.
Results may differ from a plain program's by a relative error of at most 0.0033.
Values may be sent and summed in bfloat16 or wider, within the bound.
A program may use at most 64 MiB of HBM per device.

v0:
```python
import jax
import jax.numpy as jnp
from jax import lax
from jax.sharding import PartitionSpec as P

RANGE = 8


def extended_2(cells, sides, width):
    for axis, dim in sides:
        count = lax.axis_size(axis)
        head = lax.slice_in_dim(cells, 0, width, axis=dim)
        tail = lax.slice_in_dim(cells, cells.shape[dim] - width, cells.shape[dim], axis=dim)
        cells = jnp.concatenate(
            [
                lax.ppermute(tail, axis, [(i, (i + 1) % count) for i in range(count)]),
                cells,
                lax.ppermute(head, axis, [((i + 1) % count, i) for i in range(count)]),
            ],
            axis=dim,
        )
    return cells


def partner(block, axis, distance):
    count = lax.axis_size(axis)
    route = []
    for low in range(count):
        high = low | 1 << distance
        if high != low and high < count:
            route += [(low, high), (high, low)]
    return lax.ppermute(block, axis, route)


def inner_rows(left_rows, right_rows):
    return lax.dot_general(
        left_rows, right_rows, (((1,), (1,)), ((), ())), precision=lax.Precision.HIGHEST
    )


def times_rows(coef_matrix, span_rows):
    return lax.dot_general(
        coef_matrix, span_rows, (((0,), (0,)), ((), ())), precision=lax.Precision.HIGHEST
    )


def small_product(left_matrix, right_matrix):
    return jnp.dot(left_matrix, right_matrix, precision=lax.Precision.HIGHEST)


def per_device(
    vectors, basis, potential, hop_table, soc_table, nbr_block, nbr_type, nbr_count, flip_block
):
    block_local = nbr_block.shape[0]
    block_width = hop_table.shape[1]
    type_total = hop_table.shape[0]
    slot_total = nbr_block.shape[1]
    vector_count = vectors.shape[1]
    domain_total = lax.axis_size("dom")
    block_total = block_local * domain_total
    norm_count = float(2 * block_local * block_width * domain_total)
    first_block = lax.axis_index("dom") * block_local
    spin_index = lax.axis_index("spin")
    local_index = jnp.arange(block_local, dtype=jnp.int32)
    offset = (nbr_block - (first_block + local_index)[:, None] + RANGE) % block_total - RANGE
    flat_index = (local_index[:, None] + RANGE + offset) * type_total + nbr_type
    live_mask = (jnp.arange(slot_total, dtype=jnp.int32)[None, :] < nbr_count[:, None]).astype(
        jnp.float32
    )
    flip_local = flip_block - first_block
    soc_own = lax.dynamic_index_in_dim(soc_table, spin_index, 0, keepdims=False)
    onsite = potential[0]

    def apply_operator(field):
        rounded = field.reshape(vector_count, block_local, block_width).astype(jnp.bfloat16)
        extended = extended_2(rounded, (("dom", 1),), RANGE)
        products = jnp.einsum(
            "kjc,tbc->kjtb", extended, hop_table, preferred_element_type=jnp.float32
        )
        products = products.reshape(vector_count, -1, block_width)
        gathered = jnp.take(products, flat_index.reshape(-1), axis=1)
        gathered = gathered.reshape(vector_count, block_local, slot_total, block_width)
        hopping = jnp.sum(gathered * live_mask[None, :, :, None], axis=2)
        other_side = partner(rounded, "spin", 0)
        picked = jnp.take(other_side, flip_local, axis=1)
        flip_term = jnp.einsum("kic,bc->kib", picked, soc_own, preferred_element_type=jnp.float32)
        return onsite[None, :] * field + (hopping + flip_term).reshape(vector_count, -1)

    def orthonormal(span, image):
        span_gram, correlation, image_gram = lax.psum(
            (inner_rows(span, span), inner_rows(span, image), inner_rows(image, image)),
            ("dom", "spin"),
        )
        span_gram = span_gram / norm_count
        first_coef = correlation / norm_count
        image_gram = image_gram / norm_count
        total_coef = 2.0 * first_coef - small_product(span_gram, first_coef)
        twice = image - times_rows(total_coef, span)
        gram_matrix = (
            image_gram
            - small_product(total_coef.T, first_coef)
            - small_product(first_coef.T, total_coef)
            + small_product(total_coef.T, small_product(span_gram, total_coef))
        )
        lower_factor = jnp.linalg.cholesky(gram_matrix)
        new_block = lax.linalg.triangular_solve(lower_factor, twice, left_side=True, lower=True)
        coefs = jnp.concatenate([total_coef, lower_factor.T], axis=0)
        return (new_block, coefs)

    current = vectors[0]
    span = jnp.concatenate([basis[0], current], axis=0)
    block_one, coefs_one = orthonormal(span, apply_operator(current))
    span_two = jnp.concatenate([span, block_one], axis=0)
    block_two, coefs_two = orthonormal(span_two, apply_operator(block_one))
    return (block_one[None], block_two[None], coefs_one, coefs_two)


def solution(mesh):
    return jax.shard_map(
        per_device,
        mesh=mesh,
        in_specs=(
            P("spin", None, "dom"),
            P("spin", None, "dom"),
            P("spin", "dom"),
            P(),
            P(),
            P("dom", None),
            P("dom", None),
            P("dom"),
            P("dom"),
        ),
        out_specs=(P("spin", None, "dom"), P("spin", None, "dom"), P(), P()),
        check_vma=False,
    )
```

profile of v0, /device:TPU:0, one launch (start us, length us, event | category | flops | bytes accessed | tf_op | source)
XLA Modules:
  0.0 202.6 jit_solution(12468295660769314962)
XLA Ops:
  0.6 1.2 copy.121
  2.4 2.5 %collective-permute-start = (bf16[8,8,128]{2,1,0:T(8,128)(2,1)S(1)}, bf16[8,8,128]{2,1,0:T(8,128)(2,1)S(1)}, u32[]{:S(2)}, u32[]{:S(2)}) collective-permute-start(bf16[8,8,128]{2,1,0:T(8,128)(2,1)S(1)} %get-tuple-element.18), channel_id=1, source_target_pairs={{0,2},{2,4},{4,6},{6,8},{8,10},{10,12},{12,14},{14,16},{16,18},{18... | collective-permute-start | bytes 49160 | tf_op jit(solution)/shard_map/ppermute | solution.py:16
  5.0 4.1 %collective-permute-start.1 = (bf16[8,8,128]{2,1,0:T(8,128)(2,1)S(1)}, bf16[8,8,128]{2,1,0:T(8,128)(2,1)S(1)}, u32[]{:S(2)}, u32[]{:S(2)}) collective-permute-start(bf16[8,8,128]{2,1,0:T(8,128)(2,1)S(1)} %get-tuple-element.19), channel_id=1, source_target_pairs={{2,0},{4,2},{6,4},{8,6},{10,8},{12,10},{14,12},{16,14},{18,16},{20... | collective-permute-start | bytes 49160 | tf_op jit(solution)/shard_map/ppermute | solution.py:18
  11.9 4.2 %fusion.1 = f32[24,24]{1,0:T(8,128)} fusion(f32[8,16384]{1,0:T(8,128)} %bitcast.113, f32[16,16384]{1,0:T(8,128)} %bitcast.122), kind=kOutput, calls=%fused_computation.27 | convolution fusion | flops 113639424 | bytes 1575168 | tf_op jit(solution)/shard_map/dot_general | solution.py:36
  16.8 1.4 copy.120
  18.3 7.5 %copy.57 = f32[8,1152,128]{2,0,1:T(8,128)} copy(f32[8,1152,128]{2,1,0:T(8,128)S(1)} %bitcast.120) | data formatting | bytes 9437184 | tf_op jit(solution)/shard_map/reshape | solution.py:80
  25.8 18.1 %gather_fusion = f32[2048,8,128]{2,1,0:T(8,128)} fusion(f32[8,1152,128]{2,0,1:T(8,128)} %copy.57, s32[2048]{0:T(1024)S(1)} %fusion.43), kind=kCustom, calls=%fused_computation.clone | custom fusion | bytes 16785408 | tf_op jit(solution)/shard_map/jit(_take)/gather | solution.py:81
  43.9 9.2 %multiply_reduce_fusion.1 = f32[8,128,128]{2,0,1:T(8,128)S(1)} fusion(f32[128,16]{1,0:T(8,128)S(1)} %fusion.25, f32[2048,8,128]{2,1,0:T(8,128)} %gather_fusion, pred[2048]{0:T(1024)(128)(4,1)S(1)} %compare_and_fusion), kind=kLoop, calls=%fused_computation.8 | loop fusion | flops 6160384 | bytes 8923136 | tf_op jit(solution)/shard_map/reduce_sum | solution.py:83
  56.0 1.3 convolution_bitcast_fusion.1
  57.3 1.6 fusion.2
  59.0 38.1 %all-reduce.1 = (f32[24,24]{1,0:T(8,128)S(1)}, f32[24,8]{0,1:T(8,128)S(1)}, f32[8,8]{0,1:T(8,128)S(1)}) all-reduce(f32[24,24]{1,0:T(8,128)S(1)} %copy-done.5, f32[24,8]{0,1:T(8,128)S(1)} %fusion.2, f32[8,8]{0,1:T(8,128)S(1)} %convolution_bitcast_fusion.1), channel_id=1, replica_groups=mesh['dom'=16,'spin'=2] {'dom','spin'}, use_global_device_ids=true, to_apply=%region_3.6 | all-reduce | flops 832 | bytes 6656 | tf_op jit(solution)/shard_map/psum | solution.py:90
  102.5 2.4 %fusion.3 = f32[32,32]{1,0:T(8,128)} fusion(f32[8,16384]{1,0:T(8,128)S(1)} %fusion.47, f32[8,16384]{1,0:T(8,128)S(1)} %bitcast.117, f32[16,16384]{1,0:T(8,128)S(1)} %bitcast.125), kind=kOutput, calls=%fused_computation.29 | convolution fusion | flops 202375168 | bytes 2101248 | tf_op jit(solution)/shard_map/dot_general | solution.py:36
  104.9 2.3 %collective-permute-start.3 = (bf16[8,8,128]{2,1,0:T(8,128)(2,1)S(1)}, bf16[8,8,128]{2,1,0:T(8,128)(2,1)S(1)}, u32[]{:S(2)}, u32[]{:S(2)}) collective-permute-start(bf16[8,8,128]{2,1,0:T(8,128)(2,1)S(1)} %get-tuple-element.16), channel_id=1, source_target_pairs={{0,2},{2,4},{4,6},{6,8},{8,10},{10,12},{12,14},{14,16},{16,18},{18... | collective-permute-start | bytes 49160 | tf_op jit(solution)/shard_map/ppermute | solution.py:16
  107.2 3.3 %collective-permute-start.4 = (bf16[8,8,128]{2,1,0:T(8,128)(2,1)S(1)}, bf16[8,8,128]{2,1,0:T(8,128)(2,1)S(1)}, u32[]{:S(2)}, u32[]{:S(2)}) collective-permute-start(bf16[8,8,128]{2,1,0:T(8,128)(2,1)S(1)} %get-tuple-element.17), channel_id=1, source_target_pairs={{2,0},{4,2},{6,4},{8,6},{10,8},{12,10},{14,12},{16,14},{18,16},{20... | collective-permute-start | bytes 49160 | tf_op jit(solution)/shard_map/ppermute | solution.py:18
  113.0 1.4 copy.119
  114.4 7.5 %copy.73 = f32[8,1152,128]{2,0,1:T(8,128)} copy(f32[8,1152,128]{2,1,0:T(8,128)S(1)} %bitcast.121) | data formatting | bytes 9437184 | tf_op jit(solution)/shard_map/reshape | solution.py:80
  122.0 18.1 %gather_fusion.2 = f32[2048,8,128]{2,1,0:T(8,128)} fusion(f32[8,1152,128]{2,0,1:T(8,128)} %copy.73, s32[2048]{0:T(1024)S(1)} %fusion.43), kind=kCustom, calls=%fused_computation.2.clone | custom fusion | bytes 16785408 | tf_op jit(solution)/shard_map/jit(_take)/gather | solution.py:81
  140.1 9.1 %multiply_reduce_fusion = f32[8,128,128]{2,0,1:T(8,128)S(1)} fusion(f32[128,16]{1,0:T(8,128)S(1)} %fusion.25, f32[2048,8,128]{2,1,0:T(8,128)} %gather_fusion.2, pred[2048]{0:T(1024)(128)(4,1)S(1)} %compare_and_fusion), kind=kLoop, calls=%fused_computation.7 | loop fusion | flops 6160384 | bytes 8923136 | tf_op jit(solution)/shard_map/reduce_sum | solution.py:83
  149.2 1.6 gather_fusion.3
  152.1 1.3 fusion.7
  153.4 1.9 fusion.4
  155.3 40.4 %all-reduce = (f32[32,32]{1,0:T(8,128)S(1)}, f32[32,8]{0,1:T(8,128)S(1)}, f32[8,8]{0,1:T(8,128)S(1)}) all-reduce(f32[32,32]{1,0:T(8,128)S(1)} %copy-done.6, f32[32,8]{0,1:T(8,128)S(1)} %fusion.4, f32[8,8]{0,1:T(8,128)S(1)} %fusion.7), channel_id=1, replica_groups=mesh['dom'=16,'spin'=2] {'dom','spin'}, use_global_device_ids=true, to_apply=%region_9.14 | all-reduce | flops 1344 | bytes 10752 | tf_op jit(solution)/shard_map/psum | solution.py:90
  196.0 1.3 convolution_subtract_fusion
  201.2 1.4 convolution_bitcast_fusion
  (73 shorter events, 20.2 us)
Async XLA Ops:
  0.6 15.4 %copy-start = (bf16[8,128,128]{2,1,0:T(8,128)(2,1)S(1)}, bf16[8,128,128]{2,1,0:T(8,128)(2,1)}, u32[]{:S(2)}) copy-start(bf16[8,128,128]{2,1,0:T(8,128)(2,1)} %param.19) | copy-start | bytes 786436
  1.8 51.3 %collective-permute-start.2 = (bf16[8,128,128]{2,1,0:T(8,128)(2,1)S(1)}, bf16[8,128,128]{2,1,0:T(8,128)(2,1)S(1)}, u32[]{:S(2)}, u32[]{:S(2)}) collective-permute-start(bf16[8,128,128]{2,1,0:T(8,128)(2,1)S(1)} %bitcast.137), channel_id=1, source_target_pairs={{0,1},{1,0},{2,3},{3,2},{4,5},{5,4},{6,7},{7,6},{8,9},{9,8},{10,11... | collective-permute-start | bytes 786440 | tf_op jit(solution)/shard_map/ppermute | solution.py:32
  2.4 13.6 %collective-permute-start = (bf16[8,8,128]{2,1,0:T(8,128)(2,1)S(1)}, bf16[8,8,128]{2,1,0:T(8,128)(2,1)S(1)}, u32[]{:S(2)}, u32[]{:S(2)}) collective-permute-start(bf16[8,8,128]{2,1,0:T(8,128)(2,1)S(1)} %get-tuple-element.18), channel_id=1, source_target_pairs={{0,2},{2,4},{4,6},{6,8},{8,10},{10,12},{12,14},{14,16},{16,18},{18... | collective-permute-start | bytes 49160 | tf_op jit(solution)/shard_map/ppermute | solution.py:16
  5.0 11.1 %collective-permute-start.1 = (bf16[8,8,128]{2,1,0:T(8,128)(2,1)S(1)}, bf16[8,8,128]{2,1,0:T(8,128)(2,1)S(1)}, u32[]{:S(2)}, u32[]{:S(2)}) collective-permute-start(bf16[8,8,128]{2,1,0:T(8,128)(2,1)S(1)} %get-tuple-element.19), channel_id=1, source_target_pairs={{2,0},{4,2},{6,4},{8,6},{10,8},{12,10},{14,12},{16,14},{18,16},{20... | collective-permute-start | bytes 49160 | tf_op jit(solution)/shard_map/ppermute | solution.py:18
  43.9 11.0 %copy-start.1 = (f32[1,8,16384]{2,1,0:T(8,128)S(1)}, f32[1,8,16384]{2,1,0:T(8,128)}, u32[]{:S(2)}) copy-start(f32[1,8,16384]{2,1,0:T(8,128)} %param.16) | copy-start | bytes 1572868
  43.9 11.0 %copy-start.4 = (f32[1,16384]{1,0:T(1,128)S(1)}, f32[1,16384]{1,0:T(1,128)}, u32[]{:S(2)}) copy-start(f32[1,16384]{1,0:T(1,128)} %param.18) | copy-start | bytes 196612
  53.3 4.0 %copy-start.2 = (f32[1,16,16384]{2,1,0:T(8,128)S(1)}, f32[1,16,16384]{2,1,0:T(8,128)}, u32[]{:S(2)}) copy-start(f32[1,16,16384]{2,1,0:T(8,128)} %param.17) | copy-start | bytes 3145732
  54.9 4.0 %copy-start.5 = (f32[24,24]{1,0:T(8,128)S(1)}, f32[24,24]{1,0:T(8,128)}, u32[]{:S(2)}) copy-start(f32[24,24]{1,0:T(8,128)} %fusion.1) | copy-start | bytes 6916
  102.3 93.7 %copy-start.3 = (f32[8,16384]{1,0:T(8,128)}, f32[8,16384]{1,0:T(8,128)S(1)}, u32[]{:S(2)}) copy-start(f32[8,16384]{1,0:T(8,128)S(1)} %fusion.47) | copy-start | bytes 1572868
  102.4 46.8 %collective-permute-start.5 = (bf16[8,128,128]{2,0,1:T(8,128)(2,1)S(1)}, bf16[8,128,128]{2,0,1:T(8,128)(2,1)}, u32[]{:S(2)}, u32[]{:S(2)}) collective-permute-start(bf16[8,128,128]{2,0,1:T(8,128)(2,1)S(1)} %convert_bitcast_fusion), channel_id=1, source_target_pairs={{0,1},{1,0},{2,3},{3,2},{4,5},{5,4},{6,7},{7,6},{8,9},{9,8},{10,11... | collective-permute-start | bytes 786440 | tf_op jit(solution)/shard_map/ppermute | solution.py:32
  104.9 7.3 %collective-permute-start.3 = (bf16[8,8,128]{2,1,0:T(8,128)(2,1)S(1)}, bf16[8,8,128]{2,1,0:T(8,128)(2,1)S(1)}, u32[]{:S(2)}, u32[]{:S(2)}) collective-permute-start(bf16[8,8,128]{2,1,0:T(8,128)(2,1)S(1)} %get-tuple-element.16), channel_id=1, source_target_pairs={{0,2},{2,4},{4,6},{6,8},{8,10},{10,12},{12,14},{14,16},{16,18},{18... | collective-permute-start | bytes 49160 | tf_op jit(solution)/shard_map/ppermute | solution.py:16
  107.2 5.1 %collective-permute-start.4 = (bf16[8,8,128]{2,1,0:T(8,128)(2,1)S(1)}, bf16[8,8,128]{2,1,0:T(8,128)(2,1)S(1)}, u32[]{:S(2)}, u32[]{:S(2)}) collective-permute-start(bf16[8,8,128]{2,1,0:T(8,128)(2,1)S(1)} %get-tuple-element.17), channel_id=1, source_target_pairs={{2,0},{4,2},{6,4},{8,6},{10,8},{12,10},{14,12},{16,14},{18,16},{20... | collective-permute-start | bytes 49160 | tf_op jit(solution)/shard_map/ppermute | solution.py:18
  140.1 10.8 %copy-start.7 = (pred[128]{0:T(512)(128)(4,1)S(1)}, pred[128]{0:T(512)(128)(4,1)}, u32[]{:S(2)}) copy-start(pred[128]{0:T(512)(128)(4,1)} %get-tuple-element.14) | copy-start | bytes 388
  152.1 3.2 %copy-start.6 = (f32[32,32]{1,0:T(8,128)S(1)}, f32[32,32]{1,0:T(8,128)}, u32[]{:S(2)}) copy-start(f32[32,32]{1,0:T(8,128)} %fusion.3) | copy-start | bytes 12292
where the time goes:
time: 203 us
  blocking collectives  78.6 us (39%)
  local copies, waits for them, and re-layouts  58.3 us (29%)
  other arithmetic  28.8 us (14%)
  matrix products  22.2 us (11%)
  starting transfers between devices  12.9 us (6%)
    psum x2, blocking collectives, orthonormal(): lax.psum((inner_rows(span, span), inner_rows(span, image), inner_rows(ima...  78.6 us
    gather x2, local copies, waits for them, and re-layouts, apply_operator(): gathered = jnp.take(products, flat_index.reshape(-1), axis=1)  36.3 us
    reduce_sum x2, other arithmetic, apply_operator(): hopping = jnp.sum(gathered * live_mask[None, :, :, None], axis=2)  18.3 us
    reshape x2, local copies, waits for them, and re-layouts, apply_operator(): products = products.reshape(vector_count, -1, block_width)  15.1 us
    dot_general x6, matrix products, inner_rows(): lax.dot_general(left_rows, right_rows, (((1,), (1,)), ((), ())), precisio...  12.6 us
    ppermute x2, starting transfers between devices, extended_2(): lax.ppermute(head, axis, [((i + 1) % count, i) for i in range(count)])  7.41 us
    ppermute x2, starting transfers between devices, extended_2(): lax.ppermute(tail, axis, [(i, (i + 1) % count) for i in range(count)])  4.82 us
  transfers between devices with their start and end apart: 6, of which 1 were waited for; matrix products, arithmetic and copies ran while one was open for 42% of the time, Pallas kernels for 0%

commit v1 on v0

--- a/solution.py
+++ b/solution.py
@@ -88,8 +88,10 @@
 
     def orthonormal(span, image):
         span_gram, correlation, image_gram = lax.psum(
-            (inner_rows(span, span), inner_rows(span, image), inner_rows(image, image)),
-            ("dom", "spin"),
+            lax.psum(
+                (inner_rows(span, span), inner_rows(span, image), inner_rows(image, image)), "spin"
+            ),
+            "dom",
         )
         span_gram = span_gram / norm_count
         first_coef = correlation / norm_count

time: 203 us -> 282 us (1.39)
  blocking collectives: 78.6 us -> 158 us
    psum x0 -> x2, blocking collectives: none -> 151 us  [orthonormal(): lax.psum(lax.psum((inner_rows(span, span), inner_rows(span, image), inner...]
    psum x2, blocking collectives: 78.6 us -> 6.84 us  [orthonormal(): lax.psum((inner_rows(span, span), inner_rows(span, image), inner_rows(ima...]
  transfers between devices with their start and end apart: 6 -> 6, of which waited for: 1 -> 1; matrix products, arithmetic and copies ran while one was open for 42% -> 30% of each run, Pallas kernels for 0% -> 0%
where the time goes in v1:
time: 282 us
  blocking collectives  158 us (56%)
  local copies, waits for them, and re-layouts  58.3 us (21%)
  other arithmetic  28.8 us (10%)
  matrix products  22.2 us (8%)
  starting transfers between devices  12.9 us (5%)
    psum x2, blocking collectives, orthonormal(): lax.psum(lax.psum((inner_rows(span, span), inner_rows(span, image), inner...  151 us
    gather x2, local copies, waits for them, and re-layouts, apply_operator(): gathered = jnp.take(products, flat_index.reshape(-1), axis=1)  36.3 us
    reduce_sum x2, other arithmetic, apply_operator(): hopping = jnp.sum(gathered * live_mask[None, :, :, None], axis=2)  18.3 us
    reshape x2, local copies, waits for them, and re-layouts, apply_operator(): products = products.reshape(vector_count, -1, block_width)  15.1 us
    dot_general x6, matrix products, inner_rows(): lax.dot_general(left_rows, right_rows, (((1,), (1,)), ((), ())), precisio...  12.6 us
    ppermute x2, starting transfers between devices, extended_2(): lax.ppermute(head, axis, [((i + 1) % count, i) for i in range(count)])  9.67 us
    psum x2, blocking collectives, orthonormal(): lax.psum((inner_rows(span, span), inner_rows(span, image), inner_rows(ima...  6.84 us
  transfers between devices with their start and end apart: 6, of which 1 were waited for; matrix products, arithmetic and copies ran while one was open for 30% of the time, Pallas kernels for 0%

profile of v1, /device:TPU:0, one launch (start us, length us, event | category | flops | bytes accessed | tf_op | source)
XLA Modules:
  0.0 281.6 jit_solution(2419140348103972456)
XLA Ops:
  2.4 2.5 collective-permute-start
  5.0 4.1 %collective-permute-start.1 = (bf16[8,8,128]{2,1,0:T(8,128)(2,1)S(1)}, bf16[8,8,128]{2,1,0:T(8,128)(2,1)S(1)}, u32[]{:S(2)}, u32[]{:S(2)}) collective-permute-start(bf16[8,8,128]{2,1,0:T(8,128)(2,1)S(1)} %get-tuple-element.25), channel_id=1, source_target_pairs={{2,0},{4,2},{6,4},{8,6},{10,8},{12,10},{14,12},{16,14},{18,16},{20... | collective-permute-start | bytes 49160 | tf_op jit(solution)/shard_map/ppermute | solution.py:18
  11.9 4.2 %fusion.1 = f32[24,24]{1,0:T(8,128)} fusion(f32[8,16384]{1,0:T(8,128)} %bitcast.113, f32[16,16384]{1,0:T(8,128)} %bitcast.122), kind=kOutput, calls=%fused_computation.27 | convolution fusion | flops 113639424 | bytes 1575168 | tf_op jit(solution)/shard_map/dot_general | solution.py:36
  16.8 1.4 copy.120
  18.3 7.5 %copy.57 = f32[8,1152,128]{2,0,1:T(8,128)} copy(f32[8,1152,128]{2,1,0:T(8,128)S(1)} %bitcast.120) | data formatting | bytes 9437184 | tf_op jit(solution)/shard_map/reshape | solution.py:80
  25.8 18.1 %gather_fusion = f32[2048,8,128]{2,1,0:T(8,128)} fusion(f32[8,1152,128]{2,0,1:T(8,128)} %copy.57, s32[2048]{0:T(1024)S(1)} %fusion.43), kind=kCustom, calls=%fused_computation.clone | custom fusion | bytes 16785408 | tf_op jit(solution)/shard_map/jit(_take)/gather | solution.py:81
  43.9 9.2 %multiply_reduce_fusion.1 = f32[8,128,128]{2,0,1:T(8,128)S(1)} fusion(f32[128,16]{1,0:T(8,128)S(1)} %fusion.25, f32[2048,8,128]{2,1,0:T(8,128)} %gather_fusion, pred[2048]{0:T(1024)(128)(4,1)S(1)} %compare_and_fusion), kind=kLoop, calls=%fused_computation.8 | loop fusion | flops 6160384 | bytes 8923136 | tf_op jit(solution)/shard_map/reduce_sum | solution.py:83
  56.0 1.3 convolution_bitcast_fusion.1
  57.3 1.6 fusion.2
  59.0 3.4 %all-reduce.3 = (f32[24,24]{1,0:T(8,128)S(1)}, f32[24,8]{0,1:T(8,128)S(1)}, f32[8,8]{0,1:T(8,128)S(1)}) all-reduce(f32[24,24]{1,0:T(8,128)S(1)} %copy-done.5, f32[24,8]{0,1:T(8,128)S(1)} %fusion.2, f32[8,8]{0,1:T(8,128)S(1)} %convolution_bitcast_fusion.1), channel_id=1, replica_groups=mesh['dom'=16,'spin'=2] {'spin'}, use_global_device_ids=true, to_apply=%region_5.8 | all-reduce | flops 832 | bytes 6656 | tf_op jit(solution)/shard_map/psum | solution.py:91
  62.4 73.5 %all-reduce.1 = (f32[24,24]{1,0:T(8,128)S(1)}, f32[24,8]{0,1:T(8,128)S(1)}, f32[8,8]{0,1:T(8,128)S(1)}) all-reduce(f32[24,24]{1,0:T(8,128)S(1)} %get-tuple-element.17, f32[24,8]{0,1:T(8,128)S(1)} %get-tuple-element.18, f32[8,8]{0,1:T(8,128)S(1)} %get-tuple-element.19), channel_id=1, replica_groups=mesh['dom'=16,'spin'=2] {'dom'}, use_global_device_ids=true, to_apply=%region_6.9 | all-reduce | flops 832 | bytes 6656 | tf_op jit(solution)/shard_map/psum | solution.py:90
  141.3 2.4 fusion.3
  143.7 5.6 %collective-permute-start.4 = (bf16[8,8,128]{2,1,0:T(8,128)(2,1)S(1)}, bf16[8,8,128]{2,1,0:T(8,128)(2,1)S(1)}, u32[]{:S(2)}, u32[]{:S(2)}) collective-permute-start(bf16[8,8,128]{2,1,0:T(8,128)(2,1)S(1)} %get-tuple-element.23), channel_id=1, source_target_pairs={{2,0},{4,2},{6,4},{8,6},{10,8},{12,10},{14,12},{16,14},{18,16},{20... | collective-permute-start | bytes 49160 | tf_op jit(solution)/shard_map/ppermute | solution.py:18
  151.8 1.4 copy.119
  153.2 7.5 %copy.73 = f32[8,1152,128]{2,0,1:T(8,128)} copy(f32[8,1152,128]{2,1,0:T(8,128)S(1)} %bitcast.121) | data formatting | bytes 9437184 | tf_op jit(solution)/shard_map/reshape | solution.py:80
  160.8 18.1 %gather_fusion.2 = f32[2048,8,128]{2,1,0:T(8,128)} fusion(f32[8,1152,128]{2,0,1:T(8,128)} %copy.73, s32[2048]{0:T(1024)S(1)} %fusion.43), kind=kCustom, calls=%fused_computation.2.clone | custom fusion | bytes 16785408 | tf_op jit(solution)/shard_map/jit(_take)/gather | solution.py:81
  178.9 9.1 %multiply_reduce_fusion = f32[8,128,128]{2,0,1:T(8,128)S(1)} fusion(f32[128,16]{1,0:T(8,128)S(1)} %fusion.25, f32[2048,8,128]{2,1,0:T(8,128)} %gather_fusion.2, pred[2048]{0:T(1024)(128)(4,1)S(1)} %compare_and_fusion), kind=kLoop, calls=%fused_computation.7 | loop fusion | flops 6160384 | bytes 8923136 | tf_op jit(solution)/shard_map/reduce_sum | solution.py:83
  188.1 1.6 gather_fusion.3
  190.9 1.3 fusion.7
  192.2 1.9 fusion.4
  194.1 3.4 %all-reduce.2 = (f32[32,32]{1,0:T(8,128)S(1)}, f32[32,8]{0,1:T(8,128)S(1)}, f32[8,8]{0,1:T(8,128)S(1)}) all-reduce(f32[32,32]{1,0:T(8,128)S(1)} %copy-done.6, f32[32,8]{0,1:T(8,128)S(1)} %fusion.4, f32[8,8]{0,1:T(8,128)S(1)} %fusion.7), channel_id=1, replica_groups=mesh['dom'=16,'spin'=2] {'spin'}, use_global_device_ids=true, to_apply=%region_14.19 | all-reduce | flops 1344 | bytes 10752 | tf_op jit(solution)/shard_map/psum | solution.py:91
  197.5 77.2 %all-reduce = (f32[32,32]{1,0:T(8,128)S(1)}, f32[32,8]{0,1:T(8,128)S(1)}, f32[8,8]{0,1:T(8,128)S(1)}) all-reduce(f32[32,32]{1,0:T(8,128)S(1)} %get-tuple-element.14, f32[32,8]{0,1:T(8,128)S(1)} %get-tuple-element.15, f32[8,8]{0,1:T(8,128)S(1)} %get-tuple-element.16), channel_id=1, replica_groups=mesh['dom'=16,'spin'=2] {'dom'}, use_global_device_ids=true, to_apply=%region_15.20 | all-reduce | flops 1344 | bytes 10752 | tf_op jit(solution)/shard_map/psum | solution.py:90
  275.0 1.3 convolution_subtract_fusion
  280.2 1.4 convolution_bitcast_fusion
  (75 shorter events, 21.4 us)
Async XLA Ops:
  0.6 15.4 %copy-start = (bf16[8,128,128]{2,1,0:T(8,128)(2,1)S(1)}, bf16[8,128,128]{2,1,0:T(8,128)(2,1)}, u32[]{:S(2)}) copy-start(bf16[8,128,128]{2,1,0:T(8,128)(2,1)} %param.19) | copy-start | bytes 786436
  1.8 51.3 %collective-permute-start.2 = (bf16[8,128,128]{2,1,0:T(8,128)(2,1)S(1)}, bf16[8,128,128]{2,1,0:T(8,128)(2,1)S(1)}, u32[]{:S(2)}, u32[]{:S(2)}) collective-permute-start(bf16[8,128,128]{2,1,0:T(8,128)(2,1)S(1)} %bitcast.137), channel_id=1, source_target_pairs={{0,1},{1,0},{2,3},{3,2},{4,5},{5,4},{6,7},{7,6},{8,9},{9,8},{10,11... | collective-permute-start | bytes 786440 | tf_op jit(solution)/shard_map/ppermute | solution.py:32
  2.4 13.6 %collective-permute-start = (bf16[8,8,128]{2,1,0:T(8,128)(2,1)S(1)}, bf16[8,8,128]{2,1,0:T(8,128)(2,1)S(1)}, u32[]{:S(2)}, u32[]{:S(2)}) collective-permute-start(bf16[8,8,128]{2,1,0:T(8,128)(2,1)S(1)} %get-tuple-element.24), channel_id=1, source_target_pairs={{0,2},{2,4},{4,6},{6,8},{8,10},{10,12},{12,14},{14,16},{16,18},{18... | collective-permute-start | bytes 49160 | tf_op jit(solution)/shard_map/ppermute | solution.py:16
  5.0 11.1 %collective-permute-start.1 = (bf16[8,8,128]{2,1,0:T(8,128)(2,1)S(1)}, bf16[8,8,128]{2,1,0:T(8,128)(2,1)S(1)}, u32[]{:S(2)}, u32[]{:S(2)}) collective-permute-start(bf16[8,8,128]{2,1,0:T(8,128)(2,1)S(1)} %get-tuple-element.25), channel_id=1, source_target_pairs={{2,0},{4,2},{6,4},{8,6},{10,8},{12,10},{14,12},{16,14},{18,16},{20... | collective-permute-start | bytes 49160 | tf_op jit(solution)/shard_map/ppermute | solution.py:18
  43.9 11.0 %copy-start.1 = (f32[1,8,16384]{2,1,0:T(8,128)S(1)}, f32[1,8,16384]{2,1,0:T(8,128)}, u32[]{:S(2)}) copy-start(f32[1,8,16384]{2,1,0:T(8,128)} %param.16) | copy-start | bytes 1572868
  43.9 11.0 %copy-start.4 = (f32[1,16384]{1,0:T(1,128)S(1)}, f32[1,16384]{1,0:T(1,128)}, u32[]{:S(2)}) copy-start(f32[1,16384]{1,0:T(1,128)} %param.18) | copy-start | bytes 196612
  53.3 4.0 %copy-start.2 = (f32[1,16,16384]{2,1,0:T(8,128)S(1)}, f32[1,16,16384]{2,1,0:T(8,128)}, u32[]{:S(2)}) copy-start(f32[1,16,16384]{2,1,0:T(8,128)} %param.17) | copy-start | bytes 3145732
  54.9 4.0 %copy-start.5 = (f32[24,24]{1,0:T(8,128)S(1)}, f32[24,24]{1,0:T(8,128)}, u32[]{:S(2)}) copy-start(f32[24,24]{1,0:T(8,128)} %fusion.1) | copy-start | bytes 6916
  141.1 133.9 %copy-start.3 = (f32[8,16384]{1,0:T(8,128)}, f32[8,16384]{1,0:T(8,128)S(1)}, u32[]{:S(2)}) copy-start(f32[8,16384]{1,0:T(8,128)S(1)} %fusion.47) | copy-start | bytes 1572868
  141.2 46.8 %collective-permute-start.5 = (bf16[8,128,128]{2,0,1:T(8,128)(2,1)S(1)}, bf16[8,128,128]{2,0,1:T(8,128)(2,1)}, u32[]{:S(2)}, u32[]{:S(2)}) collective-permute-start(bf16[8,128,128]{2,0,1:T(8,128)(2,1)S(1)} %convert_bitcast_fusion), channel_id=1, source_target_pairs={{0,1},{1,0},{2,3},{3,2},{4,5},{5,4},{6,7},{7,6},{8,9},{9,8},{10,11... | collective-permute-start | bytes 786440 | tf_op jit(solution)/shard_map/ppermute | solution.py:32
  143.7 7.3 %collective-permute-start.3 = (bf16[8,8,128]{2,1,0:T(8,128)(2,1)S(1)}, bf16[8,8,128]{2,1,0:T(8,128)(2,1)S(1)}, u32[]{:S(2)}, u32[]{:S(2)}) collective-permute-start(bf16[8,8,128]{2,1,0:T(8,128)(2,1)S(1)} %get-tuple-element.22), channel_id=1, source_target_pairs={{0,2},{2,4},{4,6},{6,8},{8,10},{10,12},{12,14},{14,16},{16,18},{18... | collective-permute-start | bytes 49160 | tf_op jit(solution)/shard_map/ppermute | solution.py:16
  143.7 7.3 %collective-permute-start.4 = (bf16[8,8,128]{2,1,0:T(8,128)(2,1)S(1)}, bf16[8,8,128]{2,1,0:T(8,128)(2,1)S(1)}, u32[]{:S(2)}, u32[]{:S(2)}) collective-permute-start(bf16[8,8,128]{2,1,0:T(8,128)(2,1)S(1)} %get-tuple-element.23), channel_id=1, source_target_pairs={{2,0},{4,2},{6,4},{8,6},{10,8},{12,10},{14,12},{16,14},{18,16},{20... | collective-permute-start | bytes 49160 | tf_op jit(solution)/shard_map/ppermute | solution.py:18
  178.9 10.8 %copy-start.7 = (pred[128]{0:T(512)(128)(4,1)S(1)}, pred[128]{0:T(512)(128)(4,1)}, u32[]{:S(2)}) copy-start(pred[128]{0:T(512)(128)(4,1)} %get-tuple-element.20) | copy-start | bytes 388
  190.9 3.2 %copy-start.6 = (f32[32,32]{1,0:T(8,128)S(1)}, f32[32,32]{1,0:T(8,128)}, u32[]{:S(2)}) copy-start(f32[32,32]{1,0:T(8,128)} %fusion.3) | copy-start | bytes 12292
